TPU v7x, 32 devices: a whole 2x2x4 slice. The times are simulated.
32 devices in a mesh: ia: 4 (over y, core), ja: 2 (over x), ka: 4 (over z).
Axes of the slice: x: 2, y: 2, z: 4, core: 2. Of those that a mesh axis runs over, the one named last changes fastest.
Arguments:
- block_coords: int32 [4, 2, 4, 4, 3], P('ia', 'ja', 'ka'), may hold values from 0 to 3, as said below
- live_blocks: int32 [4, 2, 4], P('ia', 'ja', 'ka'), may hold values from 1 to 4, as said below
- counts: int32 [4, 2, 4, 4, 64, 4096], P('ia', 'ja', 'ka'), may hold values from 0 to 7
- factor_a: float32 [1024, 256], P(('ia', 'ja', 'ka')), may hold values from 0.3 to 9.6
- factor_b: float32 [512, 256], P(('ja', 'ka')), may hold values from 0.05 to 8
- factor_c: float32 [1024, 256], P('ka', 'ia'), may hold values from 0.05 to 8
Outputs:
- factor_new: float32 [1024, 256], P(('ia', 'ja', 'ka'))
Inputs may be any that keep to these rules, and one draw needn't show every extreme that they name: `block_coords`: a device's slots name distinct blocks; slot 0 is always live, and every mode-1 block of the slab has a live block on some device. `live_blocks`: on some device all 4 slots are live.
All inputs are finite; a program needn't handle non-finite values.
Results may differ from a plain program's by a relative error of at most 0.00061.
Values may be sent and summed in bfloat16 or wider, within the bound.
A program may use at most 64 MiB of HBM per device.

v0:
```python
import jax
import jax.numpy as jnp
from jax import lax
from jax.sharding import PartitionSpec as P

R = 256
BS = 64
RB1 = 4
RB2 = 4
RB3 = 4
SLOTS = 4


def make_panel(rows_b, rows_c, index_j, index_k):
    piece_b = lax.dynamic_slice_in_dim(rows_b, index_j * BS, BS, 0)
    piece_c = lax.dynamic_slice_in_dim(rows_c, index_k * BS, BS, 0)
    return (piece_b[:, None, :] * piece_c[None, :, :]).reshape(BS * BS, R).astype(jnp.bfloat16)


def add_block(phi, factor_low, panel, index_i, weight, block_counts):
    block_a = lax.dynamic_slice_in_dim(factor_low, index_i * BS, BS, 0)
    model = lax.dot_general(
        block_a, panel, (((1,), (1,)), ((), ())), preferred_element_type=jnp.float32
    )
    ratio = (block_counts.astype(jnp.float32) / model).astype(jnp.bfloat16)
    part = jnp.dot(ratio, panel, preferred_element_type=jnp.float32) * weight
    old = lax.dynamic_slice_in_dim(phi, index_i * BS, BS, 0)
    return lax.dynamic_update_slice_in_dim(phi, old + part, index_i * BS, 0)


def local(block_coords, live_blocks, counts, factor_a, factor_b, factor_c):
    coords = block_coords.reshape(SLOTS, 3)
    local_counts = counts.reshape(SLOTS, BS, BS * BS)
    weights = (jnp.arange(SLOTS, dtype=jnp.int32) < live_blocks.reshape(())).astype(jnp.float32)
    rows_b = lax.all_gather(factor_b, "ka", axis=0, tiled=True)
    rows_c = lax.all_gather(factor_c, "ia", axis=1, tiled=True)
    sums_b = rows_b.reshape(RB2, BS, R).sum(axis=1)
    sums_c = rows_c.reshape(RB3, BS, R).sum(axis=1)
    pick_j = (coords[:, 1:2] == jnp.arange(RB2, dtype=jnp.int32)[None, :]).astype(jnp.float32)
    pick_k = (coords[:, 2:3] == jnp.arange(RB3, dtype=jnp.int32)[None, :]).astype(jnp.float32)
    masses = jnp.dot(pick_j, sums_b, precision=lax.Precision.HIGHEST) * jnp.dot(
        pick_k, sums_c, precision=lax.Precision.HIGHEST
    )
    pick_i = (coords[:, 0:1] == jnp.arange(RB1, dtype=jnp.int32)[None, :]).astype(
        jnp.float32
    ) * weights[:, None]
    mass_part = lax.dot_general(
        pick_i, masses, (((0,), (0,)), ((), ())), precision=lax.Precision.HIGHEST
    )
    mass = lax.psum(mass_part, ("ja", "ka"))
    mass_rows = jnp.broadcast_to(mass[:, None, :], (RB1, BS, R)).reshape(RB1 * BS, R)
    owned = factor_a.shape[0]
    first_row = lax.axis_index(("ja", "ka")) * owned
    my_mass = lax.dynamic_slice_in_dim(mass_rows, first_row, owned, 0)
    empty = jnp.zeros((RB1 * BS, R), jnp.float32)

    def accumulate(factor_low):

        def step(phi, item):
            index_i, index_j, index_k, weight, block_counts = item
            panel = make_panel(rows_b, rows_c, index_j, index_k)
            return (add_block(phi, factor_low, panel, index_i, weight, block_counts), None)

        phi, _ = lax.scan(
            step, empty, (coords[:, 0], coords[:, 1], coords[:, 2], weights, local_counts)
        )
        return phi

    whole = lax.all_gather(factor_a, ("ja", "ka"), axis=0, tiled=True)
    phi = accumulate(whole.astype(jnp.bfloat16))
    totals = lax.psum(phi, ("ja", "ka"))
    updated = whole * totals / mass_rows
    phi = accumulate(updated.astype(jnp.bfloat16))
    mine = lax.psum_scatter(phi, ("ja", "ka"), scatter_dimension=0, tiled=True)
    return lax.dynamic_slice_in_dim(updated, first_row, owned, 0) * mine / my_mass


def solution(mesh):
    placed = (
        P("ia", "ja", "ka", None, None),
        P("ia", "ja", "ka"),
        P("ia", "ja", "ka", None, None, None),
        P(("ia", "ja", "ka"), None),
        P(("ja", "ka"), None),
        P("ka", "ia"),
    )
    return jax.shard_map(
        local, mesh=mesh, in_specs=placed, out_specs=P(("ia", "ja", "ka"), None), check_vma=False
    )
```

profile of v0, /device:TPU:0, one launch (start us, length us, event | category | flops | bytes accessed | tf_op | source)
XLA Modules:
  0.0 275.6 jit_solution(7233616077265290646)
XLA Ops:
  6.5 0.8 copy.14
  7.3 0.2 slice_reduce_fusion.2
  7.5 7.5 %all_gather.11 = f32[256,256]{0,1:T(8,128)S(1)} all-gather(f32[256,64]{0,1:T(8,128)} %param.15), channel_id=1, replica_groups=mesh['ia'=4,'ja'=2,'ka'=4] {'ia'}, dimensions={1}, use_global_device_ids=true | all-gather | bytes 327680 | tf_op jit(solution)/shard_map/all_gather | solution.py:36
  15.1 14.3 %all_gather.10 = f32[256,256]{1,0:T(8,128)S(1)} all-gather(f32[64,256]{1,0:T(8,128)} %param.14), channel_id=1, replica_groups=mesh['ia'=4,'ja'=2,'ka'=4] {'ka'}, dimensions={0}, use_global_device_ids=true | all-gather | bytes 327680 | tf_op jit(solution)/shard_map/all_gather | solution.py:35
  30.1 31.8 %all_gather.9 = f32[256,256]{1,0:T(8,128)S(1)} all-gather(f32[32,256]{1,0:T(8,128)} %param.13), channel_id=1, replica_groups=mesh['ia'=4,'ja'=2,'ka'=4] {'ja','ka'}, dimensions={0}, use_global_device_ids=true | all-gather | bytes 294912 | tf_op jit(solution)/shard_map/all_gather | solution.py:69
  62.0 34.4 %while.20 = (s32[]{:T(128)}, f32[256,256]{1,0:T(8,128)S(1)}, s32[4]{0:T(128)S(1)}, s32[4,64,4096]{2,1,0:T(8,128)}, bf16[256,256]{1,0:T(8,128)(2,1)S(1)}, /*index...) while((s32[]{:T(128)}, f32[256,256]{1,0:T(8,128)S(1)}, ...), condition=%wide.region_1.0_spmd, body=%wide.region_0.0_spmd.sunk | while | flops 271351808 | bytes 7899463 | solution.py:64
  62.0 0.7 dynamic_slice.108
  63.3 0.7 dynamic_slice.109
  64.7 0.7 multiply_convert_fusion.4
  65.4 0.7 dynamic_slice.107
  66.8 0.7 dynamic_slice.110
  67.5 3.1 %fusion.52 = f32[256,256]{1,0:T(8,128)S(1)} fusion(f32[256,256]{1,0:T(8,128)S(1)} %get-tuple-element.345, s32[]{:T(128)S(6)} %select_n.33, bf16[4096,256]{1,0:T(8,128)(2,1)S(1)} %bitcast.70, s32[4,64,4096]{2,1,0:T(8,128)} %get-tuple-element.361, s32[]{:T(128)} %get-tuple-element.344, f32[]{:T(128)} %bitcast.60, ...), kind=kOutput, calls=%fused_computation.6.clone.1 | convolution fusion | flops 269254656 | bytes 5408768 | tf_op jit(solution)/shard_map/while/body/eval_jaxpr/dot_general | solution.py:26
  70.6 0.7 dynamic_slice.108
  71.9 0.7 dynamic_slice.109
  73.3 0.7 multiply_convert_fusion.4
  74.0 0.7 dynamic_slice.107
  75.4 0.7 dynamic_slice.110
  76.1 3.1 %fusion.52 = f32[256,256]{1,0:T(8,128)S(1)} fusion(f32[256,256]{1,0:T(8,128)S(1)} %get-tuple-element.345, s32[]{:T(128)S(6)} %select_n.33, bf16[4096,256]{1,0:T(8,128)(2,1)S(1)} %bitcast.70, s32[4,64,4096]{2,1,0:T(8,128)} %get-tuple-element.361, s32[]{:T(128)} %get-tuple-element.344, f32[]{:T(128)} %bitcast.60, ...), kind=kOutput, calls=%fused_computation.6.clone.1 | convolution fusion | flops 269254656 | bytes 5408768 | tf_op jit(solution)/shard_map/while/body/eval_jaxpr/dot_general | solution.py:26
  79.2 0.7 dynamic_slice.108
  80.5 0.7 dynamic_slice.109
  81.9 0.7 multiply_convert_fusion.4
  82.6 0.7 dynamic_slice.107
  84.0 0.7 dynamic_slice.110
  84.7 3.1 %fusion.52 = f32[256,256]{1,0:T(8,128)S(1)} fusion(f32[256,256]{1,0:T(8,128)S(1)} %get-tuple-element.345, s32[]{:T(128)S(6)} %select_n.33, bf16[4096,256]{1,0:T(8,128)(2,1)S(1)} %bitcast.70, s32[4,64,4096]{2,1,0:T(8,128)} %get-tuple-element.361, s32[]{:T(128)} %get-tuple-element.344, f32[]{:T(128)} %bitcast.60, ...), kind=kOutput, calls=%fused_computation.6.clone.1 | convolution fusion | flops 269254656 | bytes 5408768 | tf_op jit(solution)/shard_map/while/body/eval_jaxpr/dot_general | solution.py:26
  87.8 0.7 dynamic_slice.108
  89.2 0.7 dynamic_slice.109
  90.5 0.7 multiply_convert_fusion.4
  91.2 0.7 dynamic_slice.107
  92.6 0.7 dynamic_slice.110
  93.3 3.1 %fusion.52 = f32[256,256]{1,0:T(8,128)S(1)} fusion(f32[256,256]{1,0:T(8,128)S(1)} %get-tuple-element.345, s32[]{:T(128)S(6)} %select_n.33, bf16[4096,256]{1,0:T(8,128)(2,1)S(1)} %bitcast.70, s32[4,64,4096]{2,1,0:T(8,128)} %get-tuple-element.361, s32[]{:T(128)} %get-tuple-element.344, f32[]{:T(128)} %bitcast.60, ...), kind=kOutput, calls=%fused_computation.6.clone.1 | convolution fusion | flops 269254656 | bytes 5408768 | tf_op jit(solution)/shard_map/while/body/eval_jaxpr/dot_general | solution.py:26
  96.4 0.7 copy-done.1
  97.4 0.2 convolution_multiply_fusion
  97.6 0.3 fusion.24
  97.9 21.7 %psum.15 = f32[4,256]{1,0:T(4,128)S(1)} all-reduce(f32[4,256]{1,0:T(4,128)S(1)} %fusion.24), channel_id=1, replica_groups=mesh['ia'=4,'ja'=2,'ka'=4] {'ja','ka'}, use_global_device_ids=true, to_apply=%region_5.6 | all-reduce | flops 1024 | bytes 8192 | tf_op jit(solution)/shard_map/psum | solution.py:50
  119.5 49.9 %all-reduce.2.cloned.1.call-done = f32[256,256]{1,0:T(8,128)} async-done(((f32[256,256]{1,0:T(8,128)}), f32[256,256]{1,0:T(8,128)}) %all-reduce.2.cloned.1.call-update) | async-done | bytes 262160 | tf_op jit(solution)/shard_map/psum | solution.py:71
  169.4 1.0 fusion.33
  170.5 34.4 %while.21 = (s32[]{:T(128)}, f32[256,256]{1,0:T(8,128)S(1)}, s32[4]{0:T(128)S(1)}, s32[4,64,4096]{2,1,0:T(8,128)}, bf16[256,256]{1,0:T(8,128)(2,1)S(1)}, /*index...) while((s32[]{:T(128)}, f32[256,256]{1,0:T(8,128)S(1)}, ...), condition=%wide.region_7.8_spmd, body=%wide.region_6.7_spmd.sunk | while | flops 271351808 | bytes 7899463 | solution.py:64
  170.5 0.7 dynamic_slice.116
  171.8 0.7 dynamic_slice.117
  173.2 0.7 multiply_convert_fusion.5
  173.9 0.7 dynamic_slice.115
  175.3 0.7 dynamic_slice.118
  176.0 3.1 %fusion.56 = f32[256,256]{1,0:T(8,128)S(1)} fusion(f32[256,256]{1,0:T(8,128)S(1)} %get-tuple-element.387, s32[]{:T(128)S(6)} %select_n.36, bf16[4096,256]{1,0:T(8,128)(2,1)S(1)} %bitcast.71, s32[4,64,4096]{2,1,0:T(8,128)} %get-tuple-element.403, s32[]{:T(128)} %get-tuple-element.386, f32[]{:T(128)} %bitcast.68, ...), kind=kOutput, calls=%fused_computation.20.clone.1 | convolution fusion | flops 269254656 | bytes 5408768 | tf_op jit(solution)/shard_map/while/body/eval_jaxpr/dot_general | solution.py:26
  179.1 0.7 dynamic_slice.116
  180.4 0.7 dynamic_slice.117
  181.8 0.7 multiply_convert_fusion.5
  182.5 0.7 dynamic_slice.115
  183.9 0.7 dynamic_slice.118
  184.6 3.1 %fusion.56 = f32[256,256]{1,0:T(8,128)S(1)} fusion(f32[256,256]{1,0:T(8,128)S(1)} %get-tuple-element.387, s32[]{:T(128)S(6)} %select_n.36, bf16[4096,256]{1,0:T(8,128)(2,1)S(1)} %bitcast.71, s32[4,64,4096]{2,1,0:T(8,128)} %get-tuple-element.403, s32[]{:T(128)} %get-tuple-element.386, f32[]{:T(128)} %bitcast.68, ...), kind=kOutput, calls=%fused_computation.20.clone.1 | convolution fusion | flops 269254656 | bytes 5408768 | tf_op jit(solution)/shard_map/while/body/eval_jaxpr/dot_general | solution.py:26
  187.7 0.7 dynamic_slice.116
  189.0 0.7 dynamic_slice.117
  190.4 0.7 multiply_convert_fusion.5
  191.1 0.7 dynamic_slice.115
  192.5 0.7 dynamic_slice.118
  193.2 3.1 %fusion.56 = f32[256,256]{1,0:T(8,128)S(1)} fusion(f32[256,256]{1,0:T(8,128)S(1)} %get-tuple-element.387, s32[]{:T(128)S(6)} %select_n.36, bf16[4096,256]{1,0:T(8,128)(2,1)S(1)} %bitcast.71, s32[4,64,4096]{2,1,0:T(8,128)} %get-tuple-element.403, s32[]{:T(128)} %get-tuple-element.386, f32[]{:T(128)} %bitcast.68, ...), kind=kOutput, calls=%fused_computation.20.clone.1 | convolution fusion | flops 269254656 | bytes 5408768 | tf_op jit(solution)/shard_map/while/body/eval_jaxpr/dot_general | solution.py:26
  196.3 0.7 dynamic_slice.116
  197.6 0.7 dynamic_slice.117
  199.0 0.7 multiply_convert_fusion.5
  199.7 0.7 dynamic_slice.115
  201.1 0.7 dynamic_slice.118
  201.8 3.1 %fusion.56 = f32[256,256]{1,0:T(8,128)S(1)} fusion(f32[256,256]{1,0:T(8,128)S(1)} %get-tuple-element.387, s32[]{:T(128)S(6)} %select_n.36, bf16[4096,256]{1,0:T(8,128)(2,1)S(1)} %bitcast.71, s32[4,64,4096]{2,1,0:T(8,128)} %get-tuple-element.403, s32[]{:T(128)} %get-tuple-element.386, f32[]{:T(128)} %bitcast.68, ...), kind=kOutput, calls=%fused_computation.20.clone.1 | convolution fusion | flops 269254656 | bytes 5408768 | tf_op jit(solution)/shard_map/while/body/eval_jaxpr/dot_general | solution.py:26
  204.9 0.7 copy-done
  205.6 61.8 %reduce-scatter.2.cloned.1.call-done = f32[32,256]{1,0:T(8,128)} async-done(((f32[256,256]{1,0:T(8,128)}), f32[32,256]{1,0:T(8,128)}) %reduce-scatter.2.cloned.1.call-update) | async-done | bytes 32784 | tf_op jit(solution)/shard_map/reduce_scatter | solution.py:74
  267.4 1.4 dynamic-slice_divide_fusion
  (23 shorter events, 0.7 us)
Async XLA Ops:
  6.5 162.9 %all-reduce.2.cloned.1.call-start = ((), (), s32[]{:S(2)}) async-start(), calls=%async_computation.1 | async-start | bytes 524288 | tf_op jit(solution)/shard_map/psum | solution.py:71
  96.4 0.7 copy-start.1
  97.1 170.3 %reduce-scatter.2.cloned.1.call-start = ((), (), s32[]{:S(2)}) async-start(), calls=%async_computation.2 | async-start | bytes 294912 | tf_op jit(solution)/shard_map/reduce_scatter | solution.py:74
  204.9 0.7 copy-start
Sparse Core Ops, SparseCore 0:
  97.2 72.1 all-reduce.1
  205.7 61.6 reduce-scatter.1
where the time goes:
time: 277 us; the launch traced here: 276 us
  waiting for transfers between devices  112 us (40%)
  blocking collectives  75.3 us (27%)
  matrix products  25.4 us (9%)
  local copies, waits for them, and re-layouts  24 us (9%)
  loops' own time  17.1 us (6%)
  between operations  14.1 us (5%)
  other arithmetic  7.95 us (3%)
    reduce_scatter x1, waiting for transfers between devices, local(): mine = lax.psum_scatter(phi, ('ja', 'ka'), scatter_dimension=0, tiled=True)  61.8 us
    psum x1, waiting for transfers between devices, local(): totals = lax.psum(phi, ('ja', 'ka'))  49.9 us
    all_gather x1, blocking collectives, local(): whole = lax.all_gather(factor_a, ('ja', 'ka'), axis=0, tiled=True)  31.8 us
    dot_general x8, matrix products, add_block(): part = jnp.dot(ratio, panel, preferred_element_type=jnp.float32) * weight  24.7 us
    psum x1, blocking collectives, local(): mass = lax.psum(mass_part, ('ja', 'ka'))  21.7 us
    dynamic_slice x32, local copies, waits for them, and re-layouts, accumulate(): lax.scan(step, empty, (coords[:, 0], coords[:, 1], coords[:, 2], weights,...  21.4 us
    another operation x2, loops' own time, accumulate(): lax.scan(step, empty, (coords[:, 0], coords[:, 1], coords[:, 2], weights,...  17.1 us
    all_gather x1, blocking collectives, local(): rows_b = lax.all_gather(factor_b, 'ka', axis=0, tiled=True)  14.3 us
  transfers between devices with their start and end apart: 2, of which 2 were waited for; matrix products, arithmetic and copies ran while one was open for 0% of the time, Pallas kernels for 0%

commit v1 on v0

--- a/solution.py
+++ b/solution.py
@@ -68,7 +68,7 @@
 
     whole = lax.all_gather(factor_a, ("ja", "ka"), axis=0, tiled=True)
     phi = accumulate(whole.astype(jnp.bfloat16))
-    totals = lax.psum(phi, ("ja", "ka"))
+    totals = jnp.sum(lax.all_gather(phi, ("ja", "ka")), axis=0)
     updated = whole * totals / mass_rows
     phi = accumulate(updated.astype(jnp.bfloat16))
     mine = lax.psum_scatter(phi, ("ja", "ka"), scatter_dimension=0, tiled=True)

time: 277 us -> 255 us (0.921)
  waiting for transfers between devices: 112 us -> 89 us
    psum x1 -> x0, waiting for transfers between devices: 49.9 us -> none  [local(): totals = lax.psum(phi, ('ja', 'ka'))]
    all_gather x0 -> x1, waiting for transfers between devices: none -> 27.8 us  [local(): totals = jnp.sum(lax.all_gather(phi, ('ja', 'ka')), axis=0)]
where the time goes in v1:
time: 255 us; the launch traced here: 254 us
  waiting for transfers between devices  89 us (35%)
  blocking collectives  75.4 us (30%)
  matrix products  25.4 us (10%)
  local copies, waits for them, and re-layouts  24.1 us (9%)
  loops' own time  17.1 us (7%)
  between operations  14.1 us (6%)
  other arithmetic  8.74 us (3%)
    reduce_scatter x1, waiting for transfers between devices, local(): mine = lax.psum_scatter(phi, ('ja', 'ka'), scatter_dimension=0, tiled=True)  61.1 us
    all_gather x1, blocking collectives, local(): whole = lax.all_gather(factor_a, ('ja', 'ka'), axis=0, tiled=True)  31.8 us
    all_gather x1, waiting for transfers between devices, local(): totals = jnp.sum(lax.all_gather(phi, ('ja', 'ka')), axis=0)  27.8 us
    dot_general x8, matrix products, add_block(): part = jnp.dot(ratio, panel, preferred_element_type=jnp.float32) * weight  24.7 us
    psum x1, blocking collectives, local(): mass = lax.psum(mass_part, ('ja', 'ka'))  21.8 us
    dynamic_slice x32, local copies, waits for them, and re-layouts, accumulate(): lax.scan(step, empty, (coords[:, 0], coords[:, 1], coords[:, 2], weights,...  21.4 us
    another operation x2, loops' own time, accumulate(): lax.scan(step, empty, (coords[:, 0], coords[:, 1], coords[:, 2], weights,...  17.1 us
    all_gather x1, blocking collectives, local(): rows_b = lax.all_gather(factor_b, 'ka', axis=0, tiled=True)  14.3 us
  transfers between devices with their start and end apart: 2, of which 2 were waited for; matrix products, arithmetic and copies ran while one was open for 0% of the time, Pallas kernels for 0%

profile of v1, /device:TPU:0, one launch (start us, length us, event | category | flops | bytes accessed | tf_op | source)
XLA Modules:
  0.0 253.9 jit_solution(866820324215561421)
XLA Ops:
  6.5 0.8 copy.14
  7.3 0.2 slice_reduce_fusion.2
  7.5 7.5 %all_gather.17 = f32[256,256]{0,1:T(8,128)S(1)} all-gather(f32[256,64]{0,1:T(8,128)} %param.15), channel_id=1, replica_groups=mesh['ia'=4,'ja'=2,'ka'=4] {'ia'}, dimensions={1}, use_global_device_ids=true | all-gather | bytes 327680 | tf_op jit(solution)/shard_map/all_gather | solution.py:36
  15.1 14.3 %all_gather.16 = f32[256,256]{1,0:T(8,128)S(1)} all-gather(f32[64,256]{1,0:T(8,128)} %param.14), channel_id=1, replica_groups=mesh['ia'=4,'ja'=2,'ka'=4] {'ka'}, dimensions={0}, use_global_device_ids=true | all-gather | bytes 327680 | tf_op jit(solution)/shard_map/all_gather | solution.py:35
  30.1 31.8 %all_gather.15 = f32[256,256]{1,0:T(8,128)S(1)} all-gather(f32[32,256]{1,0:T(8,128)} %param.13), channel_id=1, replica_groups=mesh['ia'=4,'ja'=2,'ka'=4] {'ja','ka'}, dimensions={0}, use_global_device_ids=true | all-gather | bytes 294912 | tf_op jit(solution)/shard_map/all_gather | solution.py:69
  62.0 34.4 %while.20 = (s32[]{:T(128)}, f32[256,256]{1,0:T(8,128)S(1)}, s32[4]{0:T(128)S(1)}, s32[4,64,4096]{2,1,0:T(8,128)}, bf16[256,256]{1,0:T(8,128)(2,1)S(1)}, /*index...) while((s32[]{:T(128)}, f32[256,256]{1,0:T(8,128)S(1)}, ...), condition=%wide.region_1.0_spmd, body=%wide.region_0.0_spmd.sunk | while | flops 271351808 | bytes 7899463 | solution.py:64
  62.0 0.7 dynamic_slice.108
  63.3 0.7 dynamic_slice.109
  64.7 0.7 multiply_convert_fusion.4
  65.4 0.7 dynamic_slice.107
  66.8 0.7 dynamic_slice.110
  67.5 3.1 %fusion.52 = f32[256,256]{1,0:T(8,128)S(1)} fusion(f32[256,256]{1,0:T(8,128)S(1)} %get-tuple-element.345, s32[]{:T(128)S(6)} %select_n.33, bf16[4096,256]{1,0:T(8,128)(2,1)S(1)} %bitcast.71, s32[4,64,4096]{2,1,0:T(8,128)} %get-tuple-element.361, s32[]{:T(128)} %get-tuple-element.344, f32[]{:T(128)} %bitcast.61, ...), kind=kOutput, calls=%fused_computation.6.clone.1 | convolution fusion | flops 269254656 | bytes 5408768 | tf_op jit(solution)/shard_map/while/body/eval_jaxpr/dot_general | solution.py:26
  70.6 0.7 dynamic_slice.108
  71.9 0.7 dynamic_slice.109
  73.3 0.7 multiply_convert_fusion.4
  74.0 0.7 dynamic_slice.107
  75.4 0.7 dynamic_slice.110
  76.1 3.1 %fusion.52 = f32[256,256]{1,0:T(8,128)S(1)} fusion(f32[256,256]{1,0:T(8,128)S(1)} %get-tuple-element.345, s32[]{:T(128)S(6)} %select_n.33, bf16[4096,256]{1,0:T(8,128)(2,1)S(1)} %bitcast.71, s32[4,64,4096]{2,1,0:T(8,128)} %get-tuple-element.361, s32[]{:T(128)} %get-tuple-element.344, f32[]{:T(128)} %bitcast.61, ...), kind=kOutput, calls=%fused_computation.6.clone.1 | convolution fusion | flops 269254656 | bytes 5408768 | tf_op jit(solution)/shard_map/while/body/eval_jaxpr/dot_general | solution.py:26
  79.2 0.7 dynamic_slice.108
  80.5 0.7 dynamic_slice.109
  81.9 0.7 multiply_convert_fusion.4
  82.6 0.7 dynamic_slice.107
  84.0 0.7 dynamic_slice.110
  84.7 3.1 %fusion.52 = f32[256,256]{1,0:T(8,128)S(1)} fusion(f32[256,256]{1,0:T(8,128)S(1)} %get-tuple-element.345, s32[]{:T(128)S(6)} %select_n.33, bf16[4096,256]{1,0:T(8,128)(2,1)S(1)} %bitcast.71, s32[4,64,4096]{2,1,0:T(8,128)} %get-tuple-element.361, s32[]{:T(128)} %get-tuple-element.344, f32[]{:T(128)} %bitcast.61, ...), kind=kOutput, calls=%fused_computation.6.clone.1 | convolution fusion | flops 269254656 | bytes 5408768 | tf_op jit(solution)/shard_map/while/body/eval_jaxpr/dot_general | solution.py:26
  87.8 0.7 dynamic_slice.108
  89.2 0.7 dynamic_slice.109
  90.5 0.7 multiply_convert_fusion.4
  91.2 0.7 dynamic_slice.107
  92.6 0.7 dynamic_slice.110
  93.3 3.1 %fusion.52 = f32[256,256]{1,0:T(8,128)S(1)} fusion(f32[256,256]{1,0:T(8,128)S(1)} %get-tuple-element.345, s32[]{:T(128)S(6)} %select_n.33, bf16[4096,256]{1,0:T(8,128)(2,1)S(1)} %bitcast.71, s32[4,64,4096]{2,1,0:T(8,128)} %get-tuple-element.361, s32[]{:T(128)} %get-tuple-element.344, f32[]{:T(128)} %bitcast.61, ...), kind=kOutput, calls=%fused_computation.6.clone.1 | convolution fusion | flops 269254656 | bytes 5408768 | tf_op jit(solution)/shard_map/while/body/eval_jaxpr/dot_general | solution.py:26
  96.4 0.7 copy-done.1
  97.4 0.2 convolution_multiply_fusion
  97.6 0.3 fusion.24
  97.9 21.8 %psum.7 = f32[4,256]{1,0:T(4,128)S(1)} all-reduce(f32[4,256]{1,0:T(4,128)S(1)} %fusion.24), channel_id=1, replica_groups=mesh['ia'=4,'ja'=2,'ka'=4] {'ja','ka'}, use_global_device_ids=true, to_apply=%region_5.6 | all-reduce | flops 1024 | bytes 8192 | tf_op jit(solution)/shard_map/psum | solution.py:50
  119.7 27.8 %all-gather.3.cloned.1.call-done = f32[2048,256]{1,0:T(8,128)} async-done(((f32[256,256]{1,0:T(8,128)}), f32[2048,256]{1,0:T(8,128)}) %all-gather.3.cloned.1.call-update) | async-done | bytes 2097168 | tf_op jit(solution)/shard_map/all_gather | solution.py:71
  147.5 1.8 reduce_sum.27
  149.3 34.4 %while.21 = (s32[]{:T(128)}, f32[256,256]{1,0:T(8,128)S(1)}, s32[4]{0:T(128)S(1)}, s32[4,64,4096]{2,1,0:T(8,128)}, bf16[256,256]{1,0:T(8,128)(2,1)S(1)}, /*index...) while((s32[]{:T(128)}, f32[256,256]{1,0:T(8,128)S(1)}, ...), condition=%wide.region_7.8_spmd, body=%wide.region_6.7_spmd.sunk | while | flops 271351808 | bytes 7899463 | solution.py:64
  149.4 0.7 dynamic_slice.116
  150.7 0.7 dynamic_slice.117
  152.1 0.7 multiply_convert_fusion.5
  152.8 0.7 dynamic_slice.115
  154.2 0.7 dynamic_slice.118
  154.8 3.1 %fusion.56 = f32[256,256]{1,0:T(8,128)S(1)} fusion(f32[256,256]{1,0:T(8,128)S(1)} %get-tuple-element.387, s32[]{:T(128)S(6)} %select_n.36, bf16[4096,256]{1,0:T(8,128)(2,1)S(1)} %bitcast.72, s32[4,64,4096]{2,1,0:T(8,128)} %get-tuple-element.403, s32[]{:T(128)} %get-tuple-element.386, f32[]{:T(128)} %bitcast.69, ...), kind=kOutput, calls=%fused_computation.20.clone.1 | convolution fusion | flops 269254656 | bytes 5408768 | tf_op jit(solution)/shard_map/while/body/eval_jaxpr/dot_general | solution.py:26
  158.0 0.7 dynamic_slice.116
  159.3 0.7 dynamic_slice.117
  160.7 0.7 multiply_convert_fusion.5
  161.4 0.7 dynamic_slice.115
  162.8 0.7 dynamic_slice.118
  163.5 3.1 %fusion.56 = f32[256,256]{1,0:T(8,128)S(1)} fusion(f32[256,256]{1,0:T(8,128)S(1)} %get-tuple-element.387, s32[]{:T(128)S(6)} %select_n.36, bf16[4096,256]{1,0:T(8,128)(2,1)S(1)} %bitcast.72, s32[4,64,4096]{2,1,0:T(8,128)} %get-tuple-element.403, s32[]{:T(128)} %get-tuple-element.386, f32[]{:T(128)} %bitcast.69, ...), kind=kOutput, calls=%fused_computation.20.clone.1 | convolution fusion | flops 269254656 | bytes 5408768 | tf_op jit(solution)/shard_map/while/body/eval_jaxpr/dot_general | solution.py:26
  166.6 0.7 dynamic_slice.116
  167.9 0.7 dynamic_slice.117
  169.3 0.7 multiply_convert_fusion.5
  170.0 0.7 dynamic_slice.115
  171.4 0.7 dynamic_slice.118
  172.1 3.1 %fusion.56 = f32[256,256]{1,0:T(8,128)S(1)} fusion(f32[256,256]{1,0:T(8,128)S(1)} %get-tuple-element.387, s32[]{:T(128)S(6)} %select_n.36, bf16[4096,256]{1,0:T(8,128)(2,1)S(1)} %bitcast.72, s32[4,64,4096]{2,1,0:T(8,128)} %get-tuple-element.403, s32[]{:T(128)} %get-tuple-element.386, f32[]{:T(128)} %bitcast.69, ...), kind=kOutput, calls=%fused_computation.20.clone.1 | convolution fusion | flops 269254656 | bytes 5408768 | tf_op jit(solution)/shard_map/while/body/eval_jaxpr/dot_general | solution.py:26
  175.2 0.7 dynamic_slice.116
  176.5 0.7 dynamic_slice.117
  177.9 0.7 multiply_convert_fusion.5
  178.6 0.7 dynamic_slice.115
  180.0 0.7 dynamic_slice.118
  180.7 3.1 %fusion.56 = f32[256,256]{1,0:T(8,128)S(1)} fusion(f32[256,256]{1,0:T(8,128)S(1)} %get-tuple-element.387, s32[]{:T(128)S(6)} %select_n.36, bf16[4096,256]{1,0:T(8,128)(2,1)S(1)} %bitcast.72, s32[4,64,4096]{2,1,0:T(8,128)} %get-tuple-element.403, s32[]{:T(128)} %get-tuple-element.386, f32[]{:T(128)} %bitcast.69, ...), kind=kOutput, calls=%fused_computation.20.clone.1 | convolution fusion | flops 269254656 | bytes 5408768 | tf_op jit(solution)/shard_map/while/body/eval_jaxpr/dot_general | solution.py:26
  183.8 0.7 copy-done
  184.5 61.1 %reduce-scatter.2.cloned.1.call-done = f32[32,256]{1,0:T(8,128)} async-done(((f32[256,256]{1,0:T(8,128)}), f32[32,256]{1,0:T(8,128)}) %reduce-scatter.2.cloned.1.call-update) | async-done | bytes 32784 | tf_op jit(solution)/shard_map/reduce_scatter | solution.py:74
  245.6 1.4 dynamic-slice_divide_fusion
  (24 shorter events, 0.7 us)
Async XLA Ops:
  6.5 141.0 %all-gather.3.cloned.1.call-start = ((), (), s32[]{:S(2)}) async-start(), calls=%async_computation.2 | async-start | bytes 2359296 | tf_op jit(solution)/shard_map/all_gather | solution.py:71
  96.4 0.7 copy-start.1
  97.1 148.5 %reduce-scatter.2.cloned.1.call-start = ((), (), s32[]{:S(2)}) async-start(), calls=%async_computation.1 | async-start | bytes 294912 | tf_op jit(solution)/shard_map/reduce_scatter | solution.py:74
  183.8 0.7 copy-start
Sparse Core Ops, SparseCore 0:
  97.3 50.2 all-gather.2
  184.6 60.9 reduce-scatter.1
